TPU v7x, 256 devices: a whole 4x4x8 slice. The times are simulated.
256 devices in a mesh: seq: 128 (over z, x, y_lo, core), sec: 2 (over y_hi).
Axes of the slice: x: 4, y: 4 (y_hi: 2, y_lo: 2; y = y_hi * 2 + y_lo), z: 8, core: 2. Of those that a mesh axis runs over, the one named last changes fastest.
Arguments:
- queries: bfloat16 [2, 2048, 64, 3072], P('sec', 'seq'), may hold values from -250 to 250
- encoded: bfloat16 [2, 1024, 32, 512], P('sec', 'seq'), may hold values from -6 to 6
- neighbours: int32 [2, 2048, 2], P('sec', 'seq'), may hold values from 0 to 1023, as said below
- kv_weight: bfloat16 [2, 512, 3072], P(None, None, 'seq'), may hold values from -0.25 to 0.25
Outputs:
- attended: bfloat16 [2, 2048, 64, 3072], P('sec', 'seq')
Inputs may be any that keep to these rules, and one draw needn't show every extreme that they name: Block id b lies on index b // 8 of seq. The spans held by one device of seq name at most 1 neighbours on any one index of seq, and in every draw some indices of seq receive exactly 1 from every device.
All inputs are finite; a program needn't handle non-finite values.
Results may differ from a plain program's by a relative error of at most 0.012.
Values may be sent and summed in bfloat16 or wider, within the bound.
No kernel may reach another device: no remote copies, remote signals or barrier semaphores. Data moves between devices by JAX's collectives and lax.ppermute only.
A program may use at most 128 MiB of HBM per device.

v0:
```python
import jax
import jax.numpy as jnp
from jax import lax
from jax.sharding import PartitionSpec as P

HDIM = 128


def from_partner(shard, axis, distance):
    return lax.ppermute(shard, axis, [(i, i ^ 1 << distance) for i in range(lax.axis_size(axis))])


def fetch_rows(block_ids, store, owners, slots_each, blocks_each):
    owner = block_ids // blocks_each
    local = block_ids % blocks_each
    owner_match = (owner[:, None] == jnp.arange(owners)[None, :]).astype(jnp.int32)
    rank = jnp.sum(jnp.cumsum(owner_match, 0) * owner_match, 1) - 1
    slot = owner * slots_each + rank
    placed = (slot[:, None] == jnp.arange(owners * slots_each)[None, :]).astype(jnp.int32)
    request = jnp.sum(placed * local[:, None], 0).reshape(owners, slots_each)
    asked = lax.all_to_all(request, "seq", split_axis=0, concat_axis=0, tiled=True)
    rows = store[asked.reshape(-1)].reshape(asked.shape + store.shape[1:])
    replies = lax.all_to_all(rows, "seq", split_axis=0, concat_axis=0, tiled=True)
    flat = replies.reshape((owners * slots_each,) + store.shape[1:])
    return flat[slot]


def body(queries, encoded, neighbours, kv_weight):
    owners = lax.axis_size("seq")
    span_count = queries.shape[1]
    blocks_each = encoded.shape[1]
    token_count = encoded.shape[2]
    width = encoded.shape[3]
    slots_each = (2 * span_count + owners - 1) // owners
    store = encoded[0]
    block_ids = neighbours[0].reshape(-1)
    remote = from_partner(store, "sec", 0)
    fetched = fetch_rows(block_ids, remote, owners, slots_each, blocks_each)
    rows = fetched.reshape(-1, width)
    piece = lax.all_gather(kv_weight, "seq", axis=2, tiled=True)
    keys = jnp.dot(rows, piece[0], preferred_element_type=jnp.float32).astype(jnp.bfloat16)
    values = jnp.dot(rows, piece[1], preferred_element_type=jnp.float32).astype(jnp.bfloat16)
    projected = jnp.stack([keys, values])
    features = queries.shape[3]
    heads = features // HDIM
    keys = projected[0].reshape(span_count, 2 * token_count, heads, HDIM)
    values = projected[1].reshape(span_count, 2 * token_count, heads, HDIM)
    query_block = queries[0].reshape(span_count, queries.shape[2], heads, HDIM)
    scores = jnp.einsum(
        "cthd,cuhd->chtu", query_block, keys, preferred_element_type=jnp.float32
    ) * HDIM ** (-0.5)
    probs = jax.nn.softmax(scores, axis=-1).astype(jnp.bfloat16)
    mixed = jnp.einsum("chtu,cuhd->cthd", probs, values, preferred_element_type=jnp.float32)
    return mixed.astype(jnp.bfloat16).reshape(1, span_count, queries.shape[2], features)


def solution(mesh):
    placed = (
        P("sec", "seq", None, None),
        P("sec", "seq", None, None),
        P("sec", "seq", None),
        P(None, None, "seq"),
    )
    return jax.shard_map(
        body, mesh=mesh, in_specs=placed, out_specs=P("sec", "seq", None, None), check_vma=False
    )
```

profile of v0, /device:TPU:98, one launch (start us, length us, event | category | flops | bytes accessed | tf_op | source)
XLA Modules:
  0.0 338.0 jit_solution(252661657235599470)
XLA Ops:
  6.5 0.7 all-gather.2.cloned.1.call-update
  7.3 0.8 copy.26
  8.2 0.2 select_reduce_fusion.1
  8.5 0.8 copy.27
  9.3 12.7 %all-to-all-start = ((s32[128,1,1]{2,1,0:T(1,128)}), s32[128,1,1]{2,1,0:T(1,128)S(1)}, u32[]{:S(2)}, u32[]{:S(2)}) async-start(s32[128,1,1]{2,1,0:T(1,128)} %copy.27), calls=%async_computation | async-start | bytes 131072 | tf_op jit(solution)/shard_map/all_to_all | solution.py:21
  22.0 3.0 collective-permute-start
  25.0 4.2 %all-to-all-done = s32[128,1,1]{2,1,0:T(1,128)S(1)} async-done(((s32[128,1,1]{2,1,0:T(1,128)}), s32[128,1,1]{2,1,0:T(1,128)S(1)}, u32[]{:S(2)}, u32[]{:S(2)}) %all-to-all-start) | async-done | bytes 544 | tf_op jit(solution)/shard_map/all_to_all | solution.py:21
  29.1 2.3 reduce
  31.5 1.1 collective-permute-done
  32.6 2.9 gather_fusion
  35.5 13.3 %all-to-all-start.1 = ((bf16[128,1,32,512]{3,2,1,0:T(8,128)(2,1)}), bf16[128,1,32,512]{3,2,1,0:T(8,128)(2,1)}, u32[]{:S(2)}, u32[]{:S(2)}) async-start(bf16[128,1,32,512]{3,2,1,0:T(8,128)(2,1)} %bitcast.55), calls=%async_computation.1 | async-start | bytes 8388608 | tf_op jit(solution)/shard_map/all_to_all | solution.py:23
  48.9 7.4 %copy.37 = bf16[128,8,24,128]{3,2,1,0:T(8,128)(2,1)} copy(bf16[128,8,24,128]{3,1,2,0:T(8,128)(2,1)} %bitcast.56) | data formatting | bytes 12582912
  56.4 99.4 %all-to-all-done.1 = bf16[128,1,32,512]{3,2,1,0:T(8,128)(2,1)} async-done(((bf16[128,1,32,512]{3,2,1,0:T(8,128)(2,1)}), bf16[128,1,32,512]{3,2,1,0:T(8,128)(2,1)}, u32[]{:S(2)}, u32[]{:S(2)}) %all-to-all-start.1) | async-done | bytes 4194336 | tf_op jit(solution)/shard_map/all_to_all | solution.py:23
  155.8 2.8 gather_fusion.1
  158.6 98.4 %all-gather.2.cloned.1.call-done = bf16[2,512,3072]{1,2,0:T(8,128)(2,1)} async-done(((bf16[2,512,24]{1,2,0:T(8,128)(2,1)}), bf16[2,512,3072]{1,2,0:T(8,128)(2,1)}) %all-gather.2.cloned.1.call-update) | async-done | bytes 6291472 | tf_op jit(solution)/shard_map/all_gather | solution.py:40
  257.0 5.6 %convert_bitcast_fusion.2 = bf16[128,8,24,128]{3,1,2,0:T(8,128)(2,1)S(1)} fusion(bf16[1024,512]{1,0:T(8,128)(2,1)S(1)} %bitcast.58, bf16[2,512,3072]{1,2,0:T(8,128)(2,1)} %all-gather.2.cloned.1.call-done), kind=kOutput, calls=%fused_computation.18 | convolution fusion | flops 3224371200 | bytes 10485760 | tf_op jit(solution)/shard_map/dot_general | solution.py:42
  262.6 4.7 %copy.35 = bf16[128,8,24,128]{3,2,1,0:T(8,128)(2,1)} copy(bf16[128,8,24,128]{3,1,2,0:T(8,128)(2,1)S(1)} %convert_bitcast_fusion.2) | data formatting | bytes 12582912
  267.3 5.9 %convert_bitcast_fusion.1 = bf16[128,8,24,128]{3,1,2,0:T(8,128)(2,1)S(1)} fusion(bf16[1024,512]{1,0:T(8,128)(2,1)S(1)} %bitcast.59, bf16[2,512,3072]{1,2,0:T(8,128)(2,1)} %all-gather.2.cloned.1.call-done), kind=kOutput, calls=%fused_computation.17 | convolution fusion | flops 3224371200 | bytes 10485760 | tf_op jit(solution)/shard_map/dot_general | solution.py:41
  273.2 4.6 %copy.36 = bf16[128,8,24,128]{3,2,1,0:T(8,128)(2,1)} copy(bf16[128,8,24,128]{3,1,2,0:T(8,128)(2,1)S(1)} %convert_bitcast_fusion.1) | data formatting | bytes 12582912
  277.8 10.8 %fusion.8 = f32[16,24,64,64]{3,2,1,0:T(8,128)} fusion(bf16[16,64,24,128]{3,2,1,0:T(8,128)(2,1)S(1)} %bitcast.53, bf16[16,64,24,128]{3,2,1,0:T(8,128)(2,1)} %bitcast.54), kind=kOutput, calls=%fused_computation.11 | convolution fusion | flops 402653184 | bytes 18874368 | tf_op jit(solution)/shard_map/cthd,cuhd->chtu/dot_general | solution.py:49
  288.5 16.3 %fusion.19 = (f32[16,24,64]{2,1,0:T(8,128)S(1)}, f32[16,24,64,64]{2,3,1,0:T(8,128)}) fusion(f32[16,24,64,64]{3,2,1,0:T(8,128)} %fusion.8), kind=kOutput, calls=%fused_computation.44 | output fusion | flops 6291519 | bytes 12681216 | tf_op jit(solution)/shard_map/sub | solution.py:52
  304.8 8.1 %convert_bitcast_fusion = bf16[16,64,24,128]{3,1,2,0:T(8,128)(2,1)S(1)} fusion(f32[16,24,64,64]{2,3,1,0:T(8,128)} %get-tuple-element.8, f32[16,24,64]{2,1,0:T(8,128)S(1)} %get-tuple-element.7, bf16[16,64,24,128]{3,2,1,0:T(8,128)(2,1)} %bitcast.57), kind=kOutput, calls=%fused_computation.14 | convolution fusion | flops 408944640 | bytes 18972672 | tf_op jit(solution)/shard_map/chtu,cuhd->cthd/dot_general | solution.py:53
  312.9 8.0 %copy.33 = bf16[16,64,24,128]{3,2,1,0:T(8,128)(2,1)} copy(bf16[16,64,24,128]{3,1,2,0:T(8,128)(2,1)S(1)} %convert_bitcast_fusion) | data formatting | bytes 12582912 | tf_op jit(solution)/shard_map/convert_element_type | solution.py:54
  320.9 10.3 %reshape.181 = bf16[1,16,64,3072]{3,2,1,0:T(8,128)(2,1)} reshape(bf16[16,64,24,128]{3,2,1,0:T(8,128)(2,1)} %copy.33) | data formatting | bytes 12582912 | tf_op jit(solution)/shard_map/reshape | solution.py:54
  (21 shorter events, 0.5 us)
Async XLA Ops:
  6.5 250.5 %all-gather.2.cloned.1.call-start = ((), (), s32[]{:S(2)}) async-start(), calls=%async_computation.2 | async-start | bytes 6340608 | tf_op jit(solution)/shard_map/all_gather | solution.py:40
  9.3 19.9 %all-to-all-start = ((s32[128,1,1]{2,1,0:T(1,128)}), s32[128,1,1]{2,1,0:T(1,128)S(1)}, u32[]{:S(2)}, u32[]{:S(2)}) async-start(s32[128,1,1]{2,1,0:T(1,128)} %copy.27), calls=%async_computation | async-start | bytes 131072 | tf_op jit(solution)/shard_map/all_to_all | solution.py:21
  22.0 10.7 %collective-permute-start = (bf16[8,32,512]{2,1,0:T(8,128)(2,1)}, bf16[8,32,512]{2,1,0:T(8,128)(2,1)S(1)}, u32[]{:S(2)}, u32[]{:S(2)}) collective-permute-start(bf16[8,32,512]{2,1,0:T(8,128)(2,1)} %bitcast.61), channel_id=1, source_target_pairs={{0,1},{1,0},{2,3},{3,2},{4,5},{5,4},{6,7},{7,6},{8,9},{9,8},{10,11... | collective-permute-start | bytes 786440 | tf_op jit(solution)/shard_map/ppermute | solution.py:10
  35.5 120.3 %all-to-all-start.1 = ((bf16[128,1,32,512]{3,2,1,0:T(8,128)(2,1)}), bf16[128,1,32,512]{3,2,1,0:T(8,128)(2,1)}, u32[]{:S(2)}, u32[]{:S(2)}) async-start(bf16[128,1,32,512]{3,2,1,0:T(8,128)(2,1)} %bitcast.55), calls=%async_computation.1 | async-start | bytes 8388608 | tf_op jit(solution)/shard_map/all_to_all | solution.py:23
  158.6 98.4 %copy-start = (bf16[32,32,512]{2,1,0:T(8,128)(2,1)}, bf16[32,32,512]{2,1,0:T(8,128)(2,1)S(1)}, u32[]{:S(2)}) copy-start(bf16[32,32,512]{2,1,0:T(8,128)(2,1)S(1)} %gather_fusion.1) | copy-start | bytes 3145732
  262.6 4.7 %copy-start.1 = (bf16[32,32,512]{2,1,0:T(8,128)(2,1)S(1)}, bf16[32,32,512]{2,1,0:T(8,128)(2,1)}, u32[]{:S(2)}) copy-start(bf16[32,32,512]{2,1,0:T(8,128)(2,1)} %copy-done) | copy-start | bytes 3145732
  262.6 15.2 %slice-start = ((s8[6291456]{0:T(1024)(128)(4,1)}), s8[4194304]{0:T(1024)(128)(4,1)S(1)}, s32[]{:S(2)}) async-start(s8[6291456]{0:T(1024)(128)(4,1)} %bitcast.51), calls=%async_computation.3 | async-start | bytes 8388608
  267.3 10.5 %slice-start.1 = ((s8[6291456]{0:T(1024)(128)(4,1)}), s8[2097152]{0:T(1024)(128)(4,1)S(1)}, s32[]{:S(2)}) async-start(s8[6291456]{0:T(1024)(128)(4,1)} %bitcast.51), calls=%async_computation.4 | async-start | bytes 4194304
Sparse Core Ops, SparseCore 0:
  9.2 247.7 all-gather.1
where the time goes:
time: 339 us; the launch traced here: 338 us
  waiting for transfers between devices  204 us (60%)
  local copies, waits for them, and re-layouts  42.4 us (13%)
  matrix products  30.4 us (9%)
  starting transfers between devices  29 us (9%)
  other arithmetic  19.1 us (6%)
  between operations  13.5 us (4%)
    all_to_all x1, waiting for transfers between devices, fetch_rows(): lax.all_to_all(rows, 'seq', split_axis=0, concat_axis=0, tiled=True)  99.4 us
    all_gather x1, waiting for transfers between devices, body(): piece = lax.all_gather(kv_weight, 'seq', axis=2, tiled=True)  98.4 us
    unnamed x12, local copies, waits for them, and re-layouts  17.4 us
    sub x1, other arithmetic, body(): probs = jax.nn.softmax(scores, axis=-1).astype(jnp.bfloat16)  16.3 us
    all_to_all x1, starting transfers between devices, fetch_rows(): lax.all_to_all(rows, 'seq', split_axis=0, concat_axis=0, tiled=True)  13.3 us
    all_to_all x1, starting transfers between devices, fetch_rows(): lax.all_to_all(request, 'seq', split_axis=0, concat_axis=0, tiled=True)  12.7 us
    dot_general x1, matrix products, body(): jnp.einsum('cthd,cuhd->chtu', query_block, keys, preferred_element_type=j...  10.8 us
    reshape x1, local copies, waits for them, and re-layouts, body(): mixed.astype(jnp.bfloat16)  10.3 us
  transfers between devices with their start and end apart: 4, of which 4 were waited for; matrix products, arithmetic and copies ran while one was open for 5% of the time, Pallas kernels for 0%

commit v1 on v0

--- a/solution.py
+++ b/solution.py
@@ -37,7 +37,10 @@
     remote = from_partner(store, "sec", 0)
     fetched = fetch_rows(block_ids, remote, owners, slots_each, blocks_each)
     rows = fetched.reshape(-1, width)
-    piece = lax.all_gather(kv_weight, "seq", axis=2, tiled=True)
+    size = lax.axis_size("seq")
+    blocks = jnp.stack([kv_weight for _ in range(size)])
+    blocks = lax.all_to_all(blocks, "seq", split_axis=0, concat_axis=0)
+    piece = jnp.concatenate(blocks, axis=2)
     keys = jnp.dot(rows, piece[0], preferred_element_type=jnp.float32).astype(jnp.bfloat16)
     values = jnp.dot(rows, piece[1], preferred_element_type=jnp.float32).astype(jnp.bfloat16)
     projected = jnp.stack([keys, values])

time: 339 us -> 366 us (1.080); the launches traced: 338 us -> 361 us
  blocking collectives: 0 us -> 105 us
  waiting for transfers between devices: 204 us -> 132 us
  between operations: 13.5 us -> 0.12 us
  local copies, waits for them, and re-layouts: 42.4 us -> 52.2 us
  matrix products: 30.4 us -> 25.6 us
    all_to_all x0 -> x1, blocking collectives: none -> 105 us  [fetch_rows(): lax.all_to_all(rows, 'seq', split_axis=0, concat_axis=0, tiled=True)]
    all_gather x1 -> x0, waiting for transfers between devices: 98.4 us -> none  [body(): piece = lax.all_gather(kv_weight, 'seq', axis=2, tiled=True)]
    all_to_all x1, waiting for transfers between devices: 99.4 us -> 127 us  [body(): blocks = lax.all_to_all(blocks, 'seq', split_axis=0, concat_axis=0)]
    unnamed x12 -> x16, local copies, waits for them, and re-layouts: 17.4 us -> 14.7 us
  transfers between devices with their start and end apart: 4 -> 3, of which waited for: 4 -> 3; matrix products, arithmetic and copies ran while one was open for 5% -> 4% of each run, Pallas kernels for 0% -> 0%
where the time goes in v1:
time: 366 us; the launch traced here: 361 us
  waiting for transfers between devices  132 us (36%)
  blocking collectives  105 us (29%)
  local copies, waits for them, and re-layouts  52.2 us (14%)
  starting transfers between devices  26.3 us (7%)
  matrix products  25.6 us (7%)
  other arithmetic  19.3 us (5%)
    all_to_all x1, waiting for transfers between devices, body(): blocks = lax.all_to_all(blocks, 'seq', split_axis=0, concat_axis=0)  127 us
    all_to_all x1, blocking collectives, fetch_rows(): lax.all_to_all(rows, 'seq', split_axis=0, concat_axis=0, tiled=True)  105 us
    sub x1, other arithmetic, body(): probs = jax.nn.softmax(scores, axis=-1).astype(jnp.bfloat16)  16.5 us
    unnamed x16, local copies, waits for them, and re-layouts  14.7 us
    all_to_all x1, starting transfers between devices, fetch_rows(): lax.all_to_all(request, 'seq', split_axis=0, concat_axis=0, tiled=True)  12.7 us
    convert_element_type x1, local copies, waits for them, and re-layouts, body(): mixed.astype(jnp.bfloat16)  10.7 us
    all_to_all x1, starting transfers between devices, body(): blocks = lax.all_to_all(blocks, 'seq', split_axis=0, concat_axis=0)  10.7 us
    dot_general x1, matrix products, body(): jnp.einsum('cthd,cuhd->chtu', query_block, keys, preferred_element_type=j...  10.7 us
  transfers between devices with their start and end apart: 3, of which 3 were waited for; matrix products, arithmetic and copies ran while one was open for 4% of the time, Pallas kernels for 0%

profile of v1, /device:TPU:98, one launch (start us, length us, event | category | flops | bytes accessed | tf_op | source)
XLA Modules:
  0.0 360.7 jit_solution(28846517541452593)
XLA Ops:
  0.0 0.8 copy.28
  2.0 12.7 %all-to-all-start = ((s32[128,1,1]{2,1,0:T(1,128)}), s32[128,1,1]{2,1,0:T(1,128)S(1)}, u32[]{:S(2)}, u32[]{:S(2)}) async-start(s32[128,1,1]{2,1,0:T(1,128)} %copy.29), calls=%async_computation | async-start | bytes 131072 | tf_op jit(solution)/shard_map/all_to_all | solution.py:21
  14.7 3.0 collective-permute-start
  17.7 4.2 %all-to-all-done = s32[128,1,1]{2,1,0:T(1,128)S(1)} async-done(((s32[128,1,1]{2,1,0:T(1,128)}), s32[128,1,1]{2,1,0:T(1,128)S(1)}, u32[]{:S(2)}, u32[]{:S(2)}) %all-to-all-start) | async-done | bytes 544 | tf_op jit(solution)/shard_map/all_to_all | solution.py:21
  21.9 2.3 reduce
  24.3 1.1 collective-permute-done
  25.4 2.8 gather_fusion
  28.2 105.2 %all_to_all.22 = bf16[128,1,32,512]{3,2,1,0:T(8,128)(2,1)} all-to-all(bf16[128,1,32,512]{3,2,1,0:T(8,128)(2,1)} %bitcast.57), channel_id=1, replica_groups=mesh['seq'=128,'sec'=2] {'seq'}, dimensions={0} | all-to-all | bytes 8388608 | tf_op jit(solution)/shard_map/all_to_all | solution.py:23
  133.4 3.4 stack.2
  136.9 10.7 %all-to-all-start.2 = ((bf16[128,2,512,24]{2,3,1,0:T(8,128)(2,1)}), bf16[128,2,512,24]{2,3,1,0:T(8,128)(2,1)}, u32[]{:S(2)}, u32[]{:S(2)}) async-start(bf16[128,2,512,24]{2,3,1,0:T(8,128)(2,1)} %stack.2), calls=%async_computation.2 | async-start | bytes 12582912 | tf_op jit(solution)/shard_map/all_to_all | solution.py:42
  147.6 7.4 %copy.40 = bf16[128,8,24,128]{3,2,1,0:T(8,128)(2,1)} copy(bf16[128,8,24,128]{3,1,2,0:T(8,128)(2,1)} %bitcast.59) | data formatting | bytes 12582912
  155.1 3.8 %gather_fusion.1 = bf16[32,32,512]{2,1,0:T(8,128)(2,1)} fusion(bf16[128,32,512]{2,1,0:T(8,128)(2,1)} %bitcast.58, s32[1024]{0:T(1024)S(1)} %pad_clamp_fusion), kind=kCustom, calls=%fused_computation.1 | custom fusion | bytes 2097280 | tf_op jit(solution)/shard_map/gather | solution.py:25
  158.9 126.5 %all-to-all-done.2 = bf16[128,2,512,24]{2,3,1,0:T(8,128)(2,1)} async-done(((bf16[128,2,512,24]{2,3,1,0:T(8,128)(2,1)}), bf16[128,2,512,24]{2,3,1,0:T(8,128)(2,1)}, u32[]{:S(2)}, u32[]{:S(2)}) %all-to-all-start.2) | async-done | bytes 6291488 | tf_op jit(solution)/shard_map/all_to_all | solution.py:42
  285.4 3.3 copy.50
  288.7 2.2 fusion.19
  291.0 3.7 %convert_bitcast_fusion.1 = bf16[128,8,24,128]{3,1,2,0:T(8,128)(2,1)S(1)} fusion(bf16[1024,512]{1,0:T(8,128)(2,1)S(1)} %bitcast.63, bf16[512,3072]{0,1:T(8,128)(2,1)S(1)} %bitcast.62), kind=kOutput, calls=%fused_computation.18 | convolution fusion | flops 3224371200 | bytes 10485760 | tf_op jit(solution)/shard_map/dot_general | solution.py:44
  294.6 4.6 %copy.39 = bf16[128,8,24,128]{3,2,1,0:T(8,128)(2,1)} copy(bf16[128,8,24,128]{3,1,2,0:T(8,128)(2,1)S(1)} %convert_bitcast_fusion.1) | data formatting | bytes 12582912
  299.3 10.7 %fusion.8 = f32[16,24,64,64]{3,2,1,0:T(8,128)} fusion(bf16[16,64,24,128]{3,2,1,0:T(8,128)(2,1)S(1)} %bitcast.55, bf16[16,64,24,128]{3,2,1,0:T(8,128)(2,1)} %bitcast.56), kind=kOutput, calls=%fused_computation.11 | convolution fusion | flops 402653184 | bytes 18874368 | tf_op jit(solution)/shard_map/cthd,cuhd->chtu/dot_general | solution.py:52
  309.9 16.5 %fusion.20 = (f32[16,24,64]{2,1,0:T(8,128)S(1)}, f32[16,24,64,64]{2,3,1,0:T(8,128)}) fusion(f32[16,24,64,64]{3,2,1,0:T(8,128)} %fusion.8), kind=kOutput, calls=%fused_computation.44 | output fusion | flops 6291519 | bytes 12681216 | tf_op jit(solution)/shard_map/sub | solution.py:55
  326.4 3.7 %convert_bitcast_fusion.2 = bf16[128,8,24,128]{3,1,2,0:T(8,128)(2,1)S(1)} fusion(bf16[1024,512]{1,0:T(8,128)(2,1)S(1)} %bitcast.64, bf16[512,3072]{0,1:T(8,128)(2,1)S(1)} %bitcast.61), kind=kOutput, calls=%fused_computation.19 | convolution fusion | flops 3224371200 | bytes 10485760 | tf_op jit(solution)/shard_map/dot_general | solution.py:45
  330.1 1.9 copy.38
  332.1 7.6 %convert_bitcast_fusion = bf16[16,64,24,128]{3,1,2,0:T(8,128)(2,1)} fusion(f32[16,24,64,64]{2,3,1,0:T(8,128)} %get-tuple-element.10, f32[16,24,64]{2,1,0:T(8,128)S(1)} %get-tuple-element.9, bf16[16,64,24,128]{3,2,1,0:T(8,128)(2,1)S(1)} %bitcast.60), kind=kOutput, calls=%fused_computation.15 | convolution fusion | flops 408944640 | bytes 18972672 | tf_op jit(solution)/shard_map/chtu,cuhd->cthd/dot_general | solution.py:56
  339.7 10.7 %copy.36 = bf16[16,64,24,128]{3,2,1,0:T(8,128)(2,1)} copy(bf16[16,64,24,128]{3,1,2,0:T(8,128)(2,1)} %convert_bitcast_fusion) | data formatting | bytes 12582912 | tf_op jit(solution)/shard_map/convert_element_type | solution.py:57
  350.4 10.3 %reshape.192 = bf16[1,16,64,3072]{3,2,1,0:T(8,128)(2,1)} reshape(bf16[16,64,24,128]{3,2,1,0:T(8,128)(2,1)} %copy.36) | data formatting | bytes 12582912 | tf_op jit(solution)/shard_map/reshape | solution.py:57
  (26 shorter events, 1.4 us)
Async XLA Ops:
  2.0 19.9 %all-to-all-start = ((s32[128,1,1]{2,1,0:T(1,128)}), s32[128,1,1]{2,1,0:T(1,128)S(1)}, u32[]{:S(2)}, u32[]{:S(2)}) async-start(s32[128,1,1]{2,1,0:T(1,128)} %copy.29), calls=%async_computation | async-start | bytes 131072 | tf_op jit(solution)/shard_map/all_to_all | solution.py:21
  14.7 10.7 %collective-permute-start = (bf16[8,32,512]{2,1,0:T(8,128)(2,1)}, bf16[8,32,512]{2,1,0:T(8,128)(2,1)S(1)}, u32[]{:S(2)}, u32[]{:S(2)}) collective-permute-start(bf16[8,32,512]{2,1,0:T(8,128)(2,1)} %bitcast.66), channel_id=1, source_target_pairs={{0,1},{1,0},{2,3},{3,2},{4,5},{5,4},{6,7},{7,6},{8,9},{9,8},{10,11... | collective-permute-start | bytes 786440 | tf_op jit(solution)/shard_map/ppermute | solution.py:10
  28.2 105.2 %copy-start.3 = (bf16[2,512,24]{1,2,0:T(8,128)(2,1)S(1)}, bf16[2,512,24]{1,2,0:T(8,128)(2,1)}, u32[]{:S(2)}) copy-start(bf16[2,512,24]{1,2,0:T(8,128)(2,1)} %param.7) | copy-start | bytes 147460
  136.9 148.5 %all-to-all-start.2 = ((bf16[128,2,512,24]{2,3,1,0:T(8,128)(2,1)}), bf16[128,2,512,24]{2,3,1,0:T(8,128)(2,1)}, u32[]{:S(2)}, u32[]{:S(2)}) async-start(bf16[128,2,512,24]{2,3,1,0:T(8,128)(2,1)} %stack.2), calls=%async_computation.2 | async-start | bytes 12582912 | tf_op jit(solution)/shard_map/all_to_all | solution.py:42
  288.7 2.3 copy-start.1
  288.7 10.5 %slice-start = ((s8[6291456]{0:T(1024)(128)(4,1)}), s8[4194304]{0:T(1024)(128)(4,1)S(1)}, s32[]{:S(2)}) async-start(s8[6291456]{0:T(1024)(128)(4,1)} %bitcast.53), calls=%async_computation.3 | async-start | bytes 8388608
  291.0 8.3 %slice-start.1 = ((s8[6291456]{0:T(1024)(128)(4,1)}), s8[2097152]{0:T(1024)(128)(4,1)S(1)}, s32[]{:S(2)}) async-start(s8[6291456]{0:T(1024)(128)(4,1)} %bitcast.53), calls=%async_computation.4 | async-start | bytes 4194304
  309.9 16.5 %copy-start = (bf16[1,512,128,24]{1,3,2,0:T(8,128)(2,1)S(1)}, bf16[1,512,128,24]{1,3,2,0:T(8,128)(2,1)}, u32[]{:S(2)}) copy-start(bf16[1,512,128,24]{1,3,2,0:T(8,128)(2,1)} %get-tuple-element.5) | copy-start | bytes 9437188
  309.9 16.5 %copy-start.2 = (bf16[32,32,512]{2,1,0:T(8,128)(2,1)S(1)}, bf16[32,32,512]{2,1,0:T(8,128)(2,1)}, u32[]{:S(2)}) copy-start(bf16[32,32,512]{2,1,0:T(8,128)(2,1)} %gather_fusion.1) | copy-start | bytes 3145732
